TPU v7x, 128 devices: a whole 4x4x4 slice. The times are simulated.
128 devices in a mesh: dp: 8 (over x, core), rows: 16 (over z, y).
Axes of the slice: x: 4, y: 4, z: 4, core: 2. Of those that a mesh axis runs over, the one named last changes fastest.
Arguments:
- item_table: float32 [524288, 128], P(('dp', 'rows')), may hold values from -3 to 3
- adagrad_state: float32 [524288, 128], P(('dp', 'rows')), may hold values from 0.0001 to 0.01
- history_ids: int32 [16384, 50], P(('dp', 'rows')), may hold values from 0 to 524287, as said below
- positive_ids: int32 [16384], P(('dp', 'rows')), may hold values from 0 to 524287, as said below
Outputs:
- new_table: float32 [524288, 128], P(('dp', 'rows'))
- new_state: float32 [524288, 128], P(('dp', 'rows'))
Inputs may be any that keep to these rules, and one draw needn't show every extreme that they name: `history_ids`: ids are counted over one device's 128 users (an aligned block of users), history and positive together, with repeats. In every such block, at most 128 ids have any one value of id // 4096, and some value has exactly 128; one value has exactly 128 in every block. Popular items repeat. `positive_ids`: counted together with history_ids as stated there.
All inputs are finite; a program needn't handle non-finite values.
Results may differ from a plain program's by a relative error of at most 0.00012.
Values sent between devices are 32-bit elements; how exact they have to be, the bound alone decides.
No kernel may reach another device: no remote copies, remote signals or barrier semaphores. Data moves between devices by JAX's collectives and lax.ppermute only.
A program may use at most 128 MiB of HBM per device.

v0:
```python
import jax
import jax.numpy as jnp
from jax import lax
from jax.sharding import Mesh
from jax.sharding import PartitionSpec as P

DP = ("dp_0", "dp_1")
ROWS = ("rows_0", "rows_1")
DP_ROWS = ("dp_0", "dp_1", "rows_0", "rows_1")
penalty_weight = 10.0
step_size = 0.05


def total_of_pieces(array, axis):
    blocks = lax.all_gather(array, axis)
    return blocks.sum(axis=0)


def one_axis_at_a_time(array, axes):
    for axis in axes:
        array = lax.psum(array, axis)
    return array


def owner_ranks(owner_dev, devices):
    total = owner_dev.shape[0]
    block = min(512, (total + 7) // 8 * 8)
    padded = (total + block - 1) // block * block
    owners_pad = jnp.concatenate([owner_dev, jnp.full((padded - total,), -1, jnp.int32)])
    owner_blocks = owners_pad.reshape(padded // block, block)
    lower = (
        jnp.arange(block, dtype=jnp.int32)[:, None] >= jnp.arange(block, dtype=jnp.int32)[None, :]
    ).astype(jnp.float32)
    columns = jnp.arange(devices, dtype=jnp.int32)[None, :]

    def step(carry, owners_blk):
        member = (owners_blk[:, None] == columns).astype(jnp.float32)
        prefix = jnp.dot(lower, member, preferred_element_type=jnp.float32)
        before = jnp.sum(member * carry[None, :], axis=1)
        ranks = jnp.sum(prefix * member, axis=1) + before - 1.0
        return (carry + jnp.sum(member, axis=0), ranks.astype(jnp.int32))

    start = jnp.zeros((devices,), jnp.float32)
    final, ranks = lax.scan(step, start, owner_blocks)
    return ranks.reshape(-1)[:total]


def shards(item_table, adagrad_state, history_ids, positive_ids):
    rows_dev, width = item_table.shape
    users_dev, hist_len = history_ids.shape
    n_data = lax.axis_size(DP)
    n_shard = lax.axis_size(ROWS)
    devices = n_data * n_shard
    requests = jnp.concatenate([history_ids, positive_ids[:, None]], axis=1).reshape(-1)
    request_count = requests.shape[0]
    capacity = max(8, (request_count * 5 // (2 * devices) + 7) // 8 * 8)
    owner_dev = requests // rows_dev
    local_row = requests % rows_dev
    slot_rank = owner_ranks(owner_dev, devices)
    flat_slot = owner_dev * capacity + slot_rank
    inverse = (
        jnp.full((devices * capacity,), request_count, jnp.int32)
        .at[flat_slot]
        .set(jnp.arange(request_count, dtype=jnp.int32))
    )
    local_pad = jnp.concatenate([local_row, jnp.full((1,), -1, jnp.int32)])
    wanted = jnp.take(local_pad, inverse, axis=0)
    item_gram = jnp.dot(
        item_table.T,
        item_table,
        precision=lax.Precision.HIGHEST,
        preferred_element_type=jnp.float32,
    )
    item_total = total_of_pieces(item_gram, DP_ROWS)
    asked = lax.all_to_all(
        wanted.reshape(devices, capacity), DP_ROWS, split_axis=0, concat_axis=0, tiled=True
    )
    present = asked >= 0
    picked = jnp.take(item_table, jnp.where(present, asked, 0), axis=0)
    fetched_rows = lax.all_to_all(
        picked * present[..., None].astype(jnp.float32),
        DP_ROWS,
        split_axis=0,
        concat_axis=0,
        tiled=True,
    )
    request_rows = jnp.take(
        fetched_rows.reshape(devices * capacity, width), flat_slot, axis=0
    ).reshape(users_dev, hist_len + 1, width)
    user_vecs = jnp.sum(request_rows[:, :hist_len], axis=1) / hist_len
    positive_vecs = request_rows[:, hist_len]
    score_gap = jnp.sum(user_vecs * positive_vecs, axis=1) - 1.0
    user_gram = jnp.dot(
        user_vecs.T, user_vecs, precision=lax.Precision.HIGHEST, preferred_element_type=jnp.float32
    )
    user_total = one_axis_at_a_time(user_gram, DP_ROWS)
    penalty_coef = penalty_weight / (rows_dev * devices)
    user_grad = 2.0 * score_gap[:, None] * positive_vecs + 2.0 * penalty_coef * jnp.dot(
        user_vecs, item_total, precision=lax.Precision.HIGHEST, preferred_element_type=jnp.float32
    )
    positive_grad = 2.0 * score_gap[:, None] * user_vecs
    per_history = jnp.broadcast_to((user_grad / hist_len)[:, None, :], (users_dev, hist_len, width))
    request_grad = jnp.concatenate([per_history, positive_grad[:, None, :]], axis=1).reshape(
        -1, width
    )
    grad_pad = jnp.concatenate([request_grad, jnp.zeros((1, width), jnp.float32)], axis=0)
    outgoing = jnp.take(grad_pad, inverse, axis=0)
    returned = lax.all_to_all(
        outgoing.reshape(devices, capacity, width), DP_ROWS, split_axis=0, concat_axis=0, tiled=True
    )
    present = asked >= 0
    target_rows = jnp.where(present, asked, 0).reshape(-1)
    masked_grad = (returned * present[..., None].astype(jnp.float32)).reshape(-1, width)
    row_grad = (
        2.0
        * penalty_coef
        * jnp.dot(
            item_table,
            user_total,
            precision=lax.Precision.HIGHEST,
            preferred_element_type=jnp.float32,
        )
    )
    row_grad = row_grad.at[target_rows].add(masked_grad)
    new_state = adagrad_state + row_grad * row_grad
    new_table = item_table - step_size * row_grad / jnp.sqrt(new_state)
    return (new_table, new_state)


def solution(mesh):
    finer = Mesh(mesh.devices.reshape(4, 2, 4, 4), ("dp_0", "dp_1", "rows_0", "rows_1"))
    placed = (P(DP_ROWS, None), P(DP_ROWS, None), P(DP_ROWS, None), P(DP_ROWS))
    return jax.shard_map(
        shards,
        mesh=finer,
        in_specs=placed,
        out_specs=(P(DP_ROWS, None), P(DP_ROWS, None)),
        check_vma=False,
    )
```

profile of v0, /device:TPU:0, one launch (start us, length us, event | category | flops | bytes accessed | tf_op | source)
XLA Modules:
  0.0 751.5 jit_solution(16251602117945407127)
XLA Ops:
  8.1 6.3 fusion.34
  14.8 7.9 %while.15 = (s32[]{:T(128)}, f32[128]{0:T(128)S(1)}, s32[13,512]{1,0:T(8,128)S(1)}, s32[13,512]{1,0:T(8,128)S(1)}, s32[]{:T(128)}, /*index=5*/s32[]{:T(128)}) while((s32[]{:T(128)}, f32[128]{0:T(128)S(1)}, s32[13,512]{1,0:T(8,128)S(1)}, s32[13,512]{1,0:T(8,128)S(1)}, s32[]{:T(128)}, /*index=5*/s32[]{:T(128)}) %tuple.43), condition=%wide.region_4.5_spmd.clone, body=%wide.region_0.4_spmd.clone.sunk | while | flops 68223744 | bytes 26200 | solution.py:44
  22.8 31.1 %scatter_custom_fusion = s32[16384]{0:T(1024)S(1)} fusion(s32[6528]{0:T(1024)S(1)} %get-tuple-element.116, s32[6528]{0:T(1024)S(1)} %iota.16, s32[]{:T(128)} %constant.135.clone.1), kind=kCustom, calls=%fused_computation.68 | custom fusion | bytes 65540 | tf_op jit(solution)/shard_map/scatter | solution.py:64
  54.0 90.5 %gather_fusion = s32[16384]{0:T(1024)S(1)} fusion(s32[6529]{0:T(1024)S(1)} %pad_add_fusion.1, s32[16384]{0:T(1024)S(1)} %fusion.20), kind=kCustom, calls=%fused_computation | custom fusion | bytes 196608 | tf_op jit(solution)/shard_map/jit(_take)/gather | solution.py:67
  144.6 20.4 %all_to_all.25 = s32[128,1,128]{2,1,0:T(1,128)S(1)} all-to-all(s32[128,1,128]{2,1,0:T(1,128)S(1)} %bitcast.55), channel_id=1, replica_groups=mesh['dp_0'=4,'dp_1'=2,'rows_0'=4,'rows_1'=4] {'dp_0','dp_1','rows_0','r..., dimensions={0} | all-to-all | bytes 131072 | tf_op jit(solution)/shard_map/all_to_all | solution.py:75
  165.1 54.4 %gather_fusion.1 = f32[16384,128]{1,0:T(8,128)} fusion(f32[4096,128]{1,0:T(8,128)S(1)} %copy-done, s32[16384]{0:T(1024)S(1)} %fusion.16), kind=kCustom, calls=%fused_computation.1 | custom fusion | bytes 16842752 | tf_op jit(solution)/shard_map/jit(_take)/gather | solution.py:79
  219.5 7.5 %select_multiply_fusion = f32[128,128,128]{2,1,0:T(8,128)} fusion(f32[128,128,128]{2,1,0:T(8,128)} %bitcast.48, f32[128,128]{1,0:T(8,128)S(1)} %get-tuple-element.114, pred[128,128]{1,0:T(8,128)(4,1)S(1)} %get-tuple-element.113), kind=kLoop, calls=%fused_computation.22 | loop fusion | flops 4194304 | bytes 16859136 | tf_op jit(solution)/shard_map/mul | solution.py:81
  227.0 5.9 all-to-all-start.1
  233.3 106.0 %all-to-all-done.1 = f32[128,128,128]{2,1,0:T(8,128)} async-done(((f32[128,128,128]{2,1,0:T(8,128)}), f32[128,128,128]{2,1,0:T(8,128)}, u32[]{:S(2)}, u32[]{:S(2)}) %all-to-all-start.1) | async-done | bytes 8388640 | tf_op jit(solution)/shard_map/all_to_all | solution.py:80
  339.3 16.3 %gather_fusion.2 = f32[6528,128]{1,0:T(8,128)} fusion(f32[16384,128]{1,0:T(8,128)} %bitcast.6, s32[7168]{0:T(1024)S(1)} %pad_clamp_fusion), kind=kCustom, calls=%fused_computation.2 | custom fusion | bytes 6710784 | tf_op jit(solution)/shard_map/jit(_take)/gather | solution.py:87
  355.6 4.6 gather.23
  373.0 4.6 reshape.204
  377.6 4.0 concatenate.19
  381.6 56.4 %gather_fusion.3 = f32[16384,128]{1,0:T(8,128)} fusion(f32[6529,128]{1,0:T(8,128)} %concatenate.19, s32[16384]{0:T(1024)S(1)} %fusion.20), kind=kCustom, calls=%fused_computation.3 | custom fusion | bytes 16842752 | tf_op jit(solution)/shard_map/jit(_take)/gather | solution.py:107
  437.9 9.9 %broadcast_select_fusion.1 = f32[128,128,128]{2,1,0:T(8,128)} fusion(f32[128,128,128]{2,1,0:T(8,128)} %bitcast.49, pred[128,128]{1,0:T(8,128)(4,1)S(1)} %bitcast.59), kind=kLoop, calls=%fused_computation.26 | loop fusion | flops 2097152 | bytes 16793600 | tf_op jit(solution)/shard_map/jit(_take)/select_n | solution.py:107
  447.9 6.1 all-to-all-start.2
  455.0 46.2 %all-reduce.7.cloned.1.call-done = f32[128,128]{1,0:T(8,128)} async-done(((f32[128,128]{1,0:T(8,128)}), f32[128,128]{1,0:T(8,128)}) %all-reduce.7.cloned.1.call-update) | async-done | bytes 65552 | tf_op jit(solution)/shard_map/psum | solution.py:21
  501.3 26.4 %all-reduce.9.cloned.1.call-done = f32[128,128]{1,0:T(8,128)} async-done(((f32[128,128]{1,0:T(8,128)}), f32[128,128]{1,0:T(8,128)}) %all-reduce.9.cloned.1.call-update) | async-done | bytes 65552 | tf_op jit(solution)/shard_map/psum | solution.py:21
  527.7 50.8 %all-reduce.11.cloned.1.call-done = f32[128,128]{1,0:T(8,128)} async-done(((f32[128,128]{1,0:T(8,128)}), f32[128,128]{1,0:T(8,128)}) %all-reduce.11.cloned.1.call-update) | async-done | bytes 65552 | tf_op jit(solution)/shard_map/psum | solution.py:21
  578.6 43.1 %all-reduce.13.cloned.1.call-done = f32[128,128]{1,0:T(8,128)} async-done(((f32[128,128]{1,0:T(8,128)}), f32[128,128]{1,0:T(8,128)}) %all-reduce.13.cloned.1.call-update) | async-done | bytes 65552 | tf_op jit(solution)/shard_map/psum | solution.py:21
  621.7 4.1 fusion.12
  628.7 7.9 %broadcast_multiply_fusion = f32[128,128,128]{2,1,0:T(8,128)} fusion(f32[128,128,128]{2,1,0:T(8,128)} %all-to-all-done.2, f32[128,128]{1,0:T(8,128)S(1)} %get-tuple-element.114), kind=kLoop, calls=%fused_computation.25 | loop fusion | flops 2097152 | bytes 16842752 | tf_op jit(solution)/shard_map/mul | solution.py:113
  636.6 102.7 %scatter_fusion = f32[4096,128]{1,0:T(8,128)} fusion(f32[4096,128]{1,0:T(8,128)} %copy.27, s32[16384]{0:T(1024)S(1)} %bitcast.53, f32[16384,128]{1,0:T(8,128)} %bitcast.47), kind=kCustom, calls=%fused_computation.5 | custom fusion | flops 2097152 | bytes 25231360 | tf_op jit(solution)/shard_map/scatter-add | solution.py:124
  739.3 4.6 multiply_subtract_fusion
  (143 shorter events, 25.1 us)
Async XLA Ops:
  8.0 6.4 copy-start.3
  8.0 6.4 copy-start.2
  8.0 357.8 %all-gather.3.cloned.1.call-start = ((), (), s32[]{:S(2)}) async-start(), calls=%async_computation.7 | async-start | bytes 8454144 | tf_op jit(solution)/shard_map/all_gather | solution.py:15
  54.0 111.0 %copy-start = (f32[4096,128]{1,0:T(8,128)S(1)}, f32[4096,128]{1,0:T(8,128)}, u32[]{:S(2)}) copy-start(f32[4096,128]{1,0:T(8,128)} %param.6) | copy-start | bytes 6291460
  227.0 112.3 %all-to-all-start.1 = ((f32[128,128,128]{2,1,0:T(8,128)}), f32[128,128,128]{2,1,0:T(8,128)}, u32[]{:S(2)}, u32[]{:S(2)}) async-start(f32[128,128,128]{2,1,0:T(8,128)} %select_multiply_fusion), calls=%async_computation.1 | async-start | bytes 16777216 | tf_op jit(solution)/shard_map/all_to_all | solution.py:80
  363.8 1.8 copy-start.1
  447.9 180.8 %all-to-all-start.2 = ((f32[128,128,128]{2,1,0:T(8,128)}), f32[128,128,128]{2,1,0:T(8,128)}, u32[]{:S(2)}, u32[]{:S(2)}) async-start(f32[128,128,128]{2,1,0:T(8,128)} %broadcast_select_fusion.1), calls=%async_computation.2 | async-start | bytes 16777216 | tf_op jit(solution)/shard_map/all_to_all | solution.py:108
  454.0 47.2 %all-reduce.7.cloned.1.call-start = ((), (), s32[]{:S(2)}) async-start(), calls=%async_computation.3 | async-start | bytes 131072 | tf_op jit(solution)/shard_map/psum | solution.py:21
  455.0 72.7 %all-reduce.9.cloned.1.call-start = ((), (), s32[]{:S(2)}) async-start(), calls=%async_computation.4 | async-start | bytes 131072 | tf_op jit(solution)/shard_map/psum | solution.py:21
  501.2 77.3 %all-reduce.11.cloned.1.call-start = ((), (), s32[]{:S(2)}) async-start(), calls=%async_computation.5 | async-start | bytes 131072 | tf_op jit(solution)/shard_map/psum | solution.py:21
  527.7 94.0 %all-reduce.13.cloned.1.call-start = ((), (), s32[]{:S(2)}) async-start(), calls=%async_computation.6 | async-start | bytes 131072 | tf_op jit(solution)/shard_map/psum | solution.py:21
Sparse Core Ops, SparseCore 0:
  14.5 72.6 all-gather.2
Sparse Core Ops, SparseCore 1:
  457.3 43.8 all-reduce.6
  503.6 24.0 all-reduce.8
  530.0 48.5 all-reduce.10
  580.8 40.8 all-reduce.12
where the time goes:
time: 753 us; the launch traced here: 752 us
  waiting for transfers between devices  273 us (36%)
  local copies, waits for them, and re-layouts  268 us (36%)
  other arithmetic  145 us (19%)
  blocking collectives  20.4 us (3%)
  matrix products  16.4 us (2%)
  between operations  16 us (2%)
  starting transfers between devices  12.3 us (2%)
    psum x4, waiting for transfers between devices, one_axis_at_a_time(): array = lax.psum(array, axis)  166 us
    all_to_all x1, waiting for transfers between devices, shards(): lax.all_to_all(picked * present[..., None].astype(jnp.float32), DP_ROWS,...  106 us
    scatter-add x1, other arithmetic, shards(): row_grad = row_grad.at[target_rows].add(masked_grad)  103 us
    gather x1, local copies, waits for them, and re-layouts, shards(): wanted = jnp.take(local_pad, inverse, axis=0)  90.5 us
    gather x1, local copies, waits for them, and re-layouts, shards(): outgoing = jnp.take(grad_pad, inverse, axis=0)  56.4 us
    gather x1, local copies, waits for them, and re-layouts, shards(): picked = jnp.take(item_table, jnp.where(present, asked, 0), axis=0)  54.4 us
    scatter x1, local copies, waits for them, and re-layouts, shards(): inverse = jnp.full((devices * capacity,), request_count, jnp.int32).at[fl...  31.1 us
    gather x2, local copies, waits for them, and re-layouts, shards(): jnp.take(fetched_rows.reshape(devices * capacity, width), flat_slot, axis=0)  20.9 us
  transfers between devices with their start and end apart: 7, of which 5 were waited for; matrix products, arithmetic and copies ran while one was open for 30% of the time, Pallas kernels for 0%

commit v1 on v0

--- a/solution.py
+++ b/solution.py
@@ -18,7 +18,8 @@
 
 def one_axis_at_a_time(array, axes):
     for axis in axes:
-        array = lax.psum(array, axis)
+        pieces = lax.all_gather(array, axis)
+        array = jnp.sum(pieces, axis=0)
     return array
 
 

time: 753 us -> 717 us (0.952)
  waiting for transfers between devices: 273 us -> 106 us
  blocking collectives: 20.4 us -> 154 us
    psum x4 -> x0, waiting for transfers between devices: 166 us -> none  [one_axis_at_a_time(): array = lax.psum(array, axis)]
    all_gather x0 -> x4, blocking collectives: none -> 134 us  [one_axis_at_a_time(): pieces = lax.all_gather(array, axis)]
  transfers between devices with their start and end apart: 7 -> 3, of which waited for: 5 -> 1; matrix products, arithmetic and copies ran while one was open for 30% -> 31% of each run, Pallas kernels for 0% -> 0%
where the time goes in v1:
time: 717 us; the launch traced here: 716 us
  local copies, waits for them, and re-layouts  268 us (37%)
  blocking collectives  154 us (21%)
  other arithmetic  145 us (20%)
  waiting for transfers between devices  106 us (15%)
  matrix products  15 us (2%)
  between operations  14.3 us (2%)
  starting transfers between devices  12.1 us (2%)
    all_gather x4, blocking collectives, one_axis_at_a_time(): pieces = lax.all_gather(array, axis)  134 us
    all_to_all x1, waiting for transfers between devices, shards(): lax.all_to_all(picked * present[..., None].astype(jnp.float32), DP_ROWS,...  106 us
    scatter-add x1, other arithmetic, shards(): row_grad = row_grad.at[target_rows].add(masked_grad)  103 us
    gather x1, local copies, waits for them, and re-layouts, shards(): wanted = jnp.take(local_pad, inverse, axis=0)  90.5 us
    gather x1, local copies, waits for them, and re-layouts, shards(): outgoing = jnp.take(grad_pad, inverse, axis=0)  56.4 us
    gather x1, local copies, waits for them, and re-layouts, shards(): picked = jnp.take(item_table, jnp.where(present, asked, 0), axis=0)  54.4 us
    scatter x1, local copies, waits for them, and re-layouts, shards(): inverse = jnp.full((devices * capacity,), request_count, jnp.int32).at[fl...  31.1 us
    gather x2, local copies, waits for them, and re-layouts, shards(): jnp.take(fetched_rows.reshape(devices * capacity, width), flat_slot, axis=0)  20.9 us
  transfers between devices with their start and end apart: 3, of which 1 were waited for; matrix products, arithmetic and copies ran while one was open for 31% of the time, Pallas kernels for 0%

profile of v1, /device:TPU:0, one launch (start us, length us, event | category | flops | bytes accessed | tf_op | source)
XLA Modules:
  0.0 715.5 jit_solution(12176099409696322764)
XLA Ops:
  7.2 6.3 fusion.34
  14.0 7.9 %while.15 = (s32[]{:T(128)}, f32[128]{0:T(128)S(1)}, s32[13,512]{1,0:T(8,128)S(1)}, s32[13,512]{1,0:T(8,128)S(1)}, s32[]{:T(128)}, /*index=5*/s32[]{:T(128)}) while((s32[]{:T(128)}, f32[128]{0:T(128)S(1)}, s32[13,512]{1,0:T(8,128)S(1)}, s32[13,512]{1,0:T(8,128)S(1)}, s32[]{:T(128)}, /*index=5*/s32[]{:T(128)}) %tuple.43), condition=%wide.region_4.5_spmd.clone, body=%wide.region_0.4_spmd.clone.sunk | while | flops 68223744 | bytes 26200 | solution.py:45
  22.0 31.1 %scatter_custom_fusion = s32[16384]{0:T(1024)S(1)} fusion(s32[6528]{0:T(1024)S(1)} %get-tuple-element.116, s32[6528]{0:T(1024)S(1)} %iota.16, s32[]{:T(128)} %constant.135.clone.1), kind=kCustom, calls=%fused_computation.68 | custom fusion | bytes 65540 | tf_op jit(solution)/shard_map/scatter | solution.py:65
  53.2 90.5 %gather_fusion = s32[16384]{0:T(1024)S(1)} fusion(s32[6529]{0:T(1024)S(1)} %pad_add_fusion.1, s32[16384]{0:T(1024)S(1)} %fusion.20), kind=kCustom, calls=%fused_computation | custom fusion | bytes 196608 | tf_op jit(solution)/shard_map/jit(_take)/gather | solution.py:68
  143.8 20.4 %all_to_all.25 = s32[128,1,128]{2,1,0:T(1,128)S(1)} all-to-all(s32[128,1,128]{2,1,0:T(1,128)S(1)} %bitcast.63), channel_id=1, replica_groups=mesh['dp_0'=4,'dp_1'=2,'rows_0'=4,'rows_1'=4] {'dp_0','dp_1','rows_0','r..., dimensions={0} | all-to-all | bytes 131072 | tf_op jit(solution)/shard_map/all_to_all | solution.py:76
  164.2 54.4 %gather_fusion.1 = f32[16384,128]{1,0:T(8,128)} fusion(f32[4096,128]{1,0:T(8,128)S(1)} %copy-done, s32[16384]{0:T(1024)S(1)} %fusion.16), kind=kCustom, calls=%fused_computation.1 | custom fusion | bytes 16842752 | tf_op jit(solution)/shard_map/jit(_take)/gather | solution.py:80
  218.7 7.5 %select_multiply_fusion = f32[128,128,128]{2,1,0:T(8,128)} fusion(f32[128,128,128]{2,1,0:T(8,128)} %bitcast.52, f32[128,128]{1,0:T(8,128)S(1)} %get-tuple-element.114, pred[128,128]{1,0:T(8,128)(4,1)S(1)} %get-tuple-element.113), kind=kLoop, calls=%fused_computation.22 | loop fusion | flops 4194304 | bytes 16859136 | tf_op jit(solution)/shard_map/mul | solution.py:82
  226.2 5.9 all-to-all-start.1
  232.5 106.0 %all-to-all-done.1 = f32[128,128,128]{2,1,0:T(8,128)} async-done(((f32[128,128,128]{2,1,0:T(8,128)}), f32[128,128,128]{2,1,0:T(8,128)}, u32[]{:S(2)}, u32[]{:S(2)}) %all-to-all-start.1) | async-done | bytes 8388640 | tf_op jit(solution)/shard_map/all_to_all | solution.py:81
  338.5 16.3 %gather_fusion.2 = f32[6528,128]{1,0:T(8,128)} fusion(f32[16384,128]{1,0:T(8,128)} %bitcast.6, s32[7168]{0:T(1024)S(1)} %pad_clamp_fusion), kind=kCustom, calls=%fused_computation.2 | custom fusion | bytes 6710784 | tf_op jit(solution)/shard_map/jit(_take)/gather | solution.py:88
  354.8 4.6 gather.23
  359.4 3.6 copy_select_fusion
  365.0 3.8 reduce_sum.107
  372.2 4.6 reshape.204
  376.8 4.0 concatenate.19
  380.7 56.4 %gather_fusion.3 = f32[16384,128]{1,0:T(8,128)} fusion(f32[6529,128]{1,0:T(8,128)} %concatenate.19, s32[16384]{0:T(1024)S(1)} %fusion.20), kind=kCustom, calls=%fused_computation.3 | custom fusion | bytes 16842752 | tf_op jit(solution)/shard_map/jit(_take)/gather | solution.py:108
  437.1 9.9 %broadcast_select_fusion.1 = f32[128,128,128]{2,1,0:T(8,128)} fusion(f32[128,128,128]{2,1,0:T(8,128)} %bitcast.53, pred[128,128]{1,0:T(8,128)(4,1)S(1)} %bitcast.67), kind=kLoop, calls=%fused_computation.26 | loop fusion | flops 2097152 | bytes 16793600 | tf_op jit(solution)/shard_map/jit(_take)/select_n | solution.py:108
  447.0 6.1 all-to-all-start.2
  453.5 103.2 %all-gather = f32[512,128]{1,0:T(8,128)S(1)} all-gather(f32[128,128]{1,0:T(8,128)S(1)} %fusion.18), channel_id=2, replica_groups=mesh['dp_0'=4,'dp_1'=2,'rows_0'=4,'rows_1'=4] {'dp_0'}, dimensions={0}, use_global_device_ids=true | all-gather | bytes 327680 | tf_op jit(solution)/shard_map/all_gather | solution.py:21
  558.7 15.0 %all-gather.2 = f32[512,128]{1,0:T(8,128)S(1)} all-gather(f32[128,128]{1,0:T(8,128)S(1)} %reduce_sum.103), channel_id=4, replica_groups=mesh['dp_0'=4,'dp_1'=2,'rows_0'=4,'rows_1'=4] {'rows_0'}, dimensions={0}, use_global_device_ids=true | all-gather | bytes 327680 | tf_op jit(solution)/shard_map/all_gather | solution.py:21
  573.7 13.5 %all-gather.3 = f32[512,128]{1,0:T(8,128)S(1)} all-gather(f32[128,128]{1,0:T(8,128)S(1)} %reduce_sum.104), channel_id=5, replica_groups=mesh['dp_0'=4,'dp_1'=2,'rows_0'=4,'rows_1'=4] {'rows_1'}, dimensions={0}, use_global_device_ids=true | all-gather | bytes 327680 | tf_op jit(solution)/shard_map/all_gather | solution.py:21
  593.4 7.9 %broadcast_multiply_fusion = f32[128,128,128]{2,1,0:T(8,128)} fusion(f32[128,128,128]{2,1,0:T(8,128)} %all-to-all-done.2, f32[128,128]{1,0:T(8,128)S(1)} %get-tuple-element.114), kind=kLoop, calls=%fused_computation.25 | loop fusion | flops 2097152 | bytes 16842752 | tf_op jit(solution)/shard_map/mul | solution.py:114
  601.3 102.7 %scatter_fusion = f32[4096,128]{1,0:T(8,128)} fusion(f32[4096,128]{1,0:T(8,128)} %copy.36, s32[16384]{0:T(1024)S(1)} %bitcast.61, f32[16384,128]{1,0:T(8,128)} %bitcast.51), kind=kCustom, calls=%fused_computation.5 | custom fusion | flops 2097152 | bytes 25231360 | tf_op jit(solution)/shard_map/scatter-add | solution.py:125
  704.0 4.6 multiply_subtract_fusion
  (139 shorter events, 22.1 us)
Async XLA Ops:
  7.2 6.4 copy-start.3
  7.2 6.4 copy-start.2
  7.2 357.8 %all-gather.7.cloned.1.call-start = ((), (), s32[]{:S(2)}) async-start(), calls=%async_computation.3 | async-start | bytes 8454144 | tf_op jit(solution)/shard_map/all_gather | solution.py:15
  53.2 111.1 %copy-start = (f32[4096,128]{1,0:T(8,128)S(1)}, f32[4096,128]{1,0:T(8,128)}, u32[]{:S(2)}) copy-start(f32[4096,128]{1,0:T(8,128)} %param.6) | copy-start | bytes 6291460
  226.2 112.3 %all-to-all-start.1 = ((f32[128,128,128]{2,1,0:T(8,128)}), f32[128,128,128]{2,1,0:T(8,128)}, u32[]{:S(2)}, u32[]{:S(2)}) async-start(f32[128,128,128]{2,1,0:T(8,128)} %select_multiply_fusion), calls=%async_computation.1 | async-start | bytes 16777216 | tf_op jit(solution)/shard_map/all_to_all | solution.py:81
  362.9 1.8 copy-start.1
  447.0 146.4 %all-to-all-start.2 = ((f32[128,128,128]{2,1,0:T(8,128)}), f32[128,128,128]{2,1,0:T(8,128)}, u32[]{:S(2)}, u32[]{:S(2)}) async-start(f32[128,128,128]{2,1,0:T(8,128)} %broadcast_select_fusion.1), calls=%async_computation.2 | async-start | bytes 16777216 | tf_op jit(solution)/shard_map/all_to_all | solution.py:109
Sparse Core Ops, SparseCore 0:
  13.7 72.6 all-gather.6
